TPU v7x, 32 devices: a whole 2x2x4 slice. The times are simulated.
32 devices in a mesh: pipe: 4 (over x, core), expert: 4 (over z), tensor: 2 (over y).
Axes of the slice: x: 2, y: 2, z: 4, core: 2. Of those that a mesh axis runs over, the one named last changes fastest.
Arguments:
- stream: bfloat16 [2, 4, 64, 7168], P(None, 'pipe', 'expert', 'tensor'), may hold values from -6 to 6
- expert_ids: int32 [2, 4, 64, 2], P(None, 'pipe', 'expert'), may hold values from 0 to 3, all different within a row; in each aligned block of 16 rows (0 to 15, 16 to 31, ..., all dimensions but the last counted through in order) at most 12 rows name the same one
- norm_gain: float32 [4, 7168], P('pipe', 'tensor'), may hold values from 0.1 to 1.9
- router: float32 [4, 7168, 4], P('pipe', 'tensor'), may hold values from -0.0625 to 0.0625
- w_up: bfloat16 [4, 7168, 1024], P('expert', 'tensor'), may hold values from -0.0625 to 0.0625
- w_down: bfloat16 [4, 1024, 7168], P('expert', None, 'tensor'), may hold values from -0.1875 to 0.1875
Outputs:
- result: bfloat16 [2, 4, 64, 7168], P(None, 'pipe', 'expert', 'tensor')
Inputs may be any that keep to these rules, and one draw needn't show every extreme that they name: `expert_ids`: each token names 2 different experts. Among the 16 tokens of one direction held by one index of the expert axis at one section, at most 12 name any one expert, and in every draw some expert is named by exactly 12 of them.
All inputs are finite; a program needn't handle non-finite values.
Results may differ from a plain program's by a relative error of at most 0.0065.
Values may be sent and summed in bfloat16 or wider, within the bound.
A program may use at most 64 MiB of HBM per device.

v0:
```python
import jax
import jax.numpy as jnp
from jax import lax
from jax.sharding import PartitionSpec as P

norm_eps = 1e-06
route_scale = 2.5


def shifted(x, axis, by):
    size = lax.axis_size(axis)
    return lax.ppermute(x, axis, [(i, (i + by) % size) for i in range(size)])


def shards(stream, expert_ids, norm_gain, router, w_up, w_down):
    ahead = shifted(stream[0], "pipe", 1)
    behind = shifted(stream[1], "pipe", -1)
    arrived = jnp.concatenate([ahead, behind], axis=0).astype(jnp.float32)
    tok_rows = arrived.shape[1]
    quarter = arrived.shape[2]
    width = float(quarter * lax.axis_size("tensor"))
    scaled = arrived * norm_gain[0]
    squares = jnp.sum(arrived * arrived, axis=-1)
    highest = lax.Precision.HIGHEST
    total_sq = lax.psum(squares, "tensor")
    inverse = lax.rsqrt(total_sq / width + norm_eps)
    normed = scaled * inverse[..., None]
    logits = lax.psum(jnp.einsum("dtc,ce->dte", normed, router[0], precision=highest), "tensor")
    chosen = expert_ids[:, 0]
    fanout = chosen.shape[2]
    experts = router.shape[2]
    capacity = 3 * tok_rows * fanout // (2 * experts)
    picked = jnp.take_along_axis(logits, chosen, axis=-1)
    scores = jax.nn.sigmoid(picked)
    gates = route_scale * scores / jnp.sum(scores, axis=-1, keepdims=True)
    onehot = (chosen[..., None] == jnp.arange(experts, dtype=jnp.int32)).astype(jnp.int32)
    onehot = onehot.reshape(2, tok_rows * fanout, experts)
    earlier = jnp.cumsum(onehot, axis=1) - onehot
    within = jnp.sum(earlier * onehot, axis=-1).reshape(chosen.shape)
    heading = lax.broadcasted_iota(jnp.int32, chosen.shape, 0)
    member = lax.broadcasted_iota(jnp.int32, chosen.shape, 1)
    target = chosen * (2 * capacity) + heading * capacity + within
    anchor = heading * tok_rows + member
    owner = (
        jnp.full((experts * 2 * capacity,), 2 * tok_rows, jnp.int32)
        .at[target.reshape(-1)]
        .set(anchor.reshape(-1))
    )
    hidden = normed.astype(jnp.bfloat16).reshape(2 * tok_rows, quarter)
    table = jnp.concatenate([hidden, jnp.zeros((1, quarter), jnp.bfloat16)], axis=0)
    outgoing = table[owner].reshape(experts, 2 * capacity, quarter)
    upper = w_up[0]
    lower = w_down[0]
    received = lax.all_to_all(outgoing, "expert", split_axis=0, concat_axis=0, tiled=True)
    senders = received.shape[0]
    count = received.shape[1]
    inner = jnp.dot(received.reshape(-1, quarter), upper, preferred_element_type=jnp.float32)
    share = lax.psum_scatter(inner, "tensor", scatter_dimension=1, tiled=True)
    active = lax.all_gather(jax.nn.silu(share).astype(jnp.bfloat16), "tensor", axis=1, tiled=True)
    produced = jnp.dot(active, lower, preferred_element_type=jnp.float32).astype(jnp.bfloat16)
    answers = lax.all_to_all(
        produced.reshape(senders, count, quarter), "expert", split_axis=0, concat_axis=0, tiled=True
    )
    flat_back = answers.reshape(experts * 2 * capacity, quarter)
    gathered = (
        flat_back[target.reshape(-1)].reshape(2, tok_rows, fanout, quarter).astype(jnp.float32)
    )
    mixed = jnp.einsum("dtk,dtkc->dtc", gates, gathered)
    result = (arrived + mixed).astype(jnp.bfloat16)
    return result[:, None]


def solution(mesh):
    return jax.shard_map(
        shards,
        mesh=mesh,
        in_specs=(
            P(None, "pipe", "expert", "tensor"),
            P(None, "pipe", "expert", None),
            P("pipe", "tensor"),
            P("pipe", "tensor", None),
            P("expert", "tensor", None),
            P("expert", None, "tensor"),
        ),
        out_specs=P(None, "pipe", "expert", "tensor"),
        check_vma=False,
    )
```

profile of v0, /device:TPU:0, one launch (start us, length us, event | category | flops | bytes accessed | tf_op | source)
XLA Modules:
  0.0 101.9 jit_solution(15306226972587400173)
XLA Ops:
  6.5 1.0 slice_bitcast_fusion.1
  7.5 0.5 collective-permute-start
  8.1 2.0 %collective-permute-start.1 = (bf16[1,16,3584]{2,1,0:T(8,128)(2,1)S(1)}, bf16[1,16,3584]{2,1,0:T(8,128)(2,1)S(1)}, u32[]{:S(2)}, u32[]{:S(2)}) collective-permute-start(bf16[1,16,3584]{2,1,0:T(8,128)(2,1)S(1)} %get-tuple-element.8), channel_id=1, source_target_pairs={{0,24},{8,0},{16,8},{24,16},{1,25},{9,1},{17,9},{25,17},{2,26},{10... | collective-permute-start | bytes 344072 | tf_op jit(solution)/shard_map/ppermute | solution.py:12
  10.0 0.8 copy.14
  10.8 0.7 broadcast_multiply_fusion
  11.7 0.2 select_reduce_fusion
  12.6 0.8 scatter_custom_fusion
  13.4 0.8 reduce
  14.3 5.2 %psum.14 = f32[2,16]{1,0:T(2,128)S(1)} all-reduce(f32[2,16]{1,0:T(2,128)S(1)} %multiply_reduce_fusion), channel_id=1, replica_groups=mesh['pipe'=4,'expert'=4,'tensor'=2] {'tensor'}, use_global_device_ids=true, to_apply=%region_1.0 | all-reduce | flops 32 | bytes 256 | tf_op jit(solution)/shard_map/psum | solution.py:25
  19.7 1.0 gather_fusion
  20.7 22.2 %all_to_all.10 = bf16[4,24,3584]{2,1,0:T(8,128)(2,1)S(1)} all-to-all(bf16[4,24,3584]{2,1,0:T(8,128)(2,1)S(1)} %bitcast.63), channel_id=1, replica_groups=mesh['pipe'=4,'expert'=4,'tensor'=2] {'expert'}, dimensions={0} | all-to-all | bytes 1376256 | tf_op jit(solution)/shard_map/all_to_all | solution.py:54
  42.8 5.1 %fusion.2 = f32[96,1024]{1,0:T(8,128)} fusion(bf16[96,3584]{1,0:T(8,128)(2,1)S(1)} %bitcast.62, bf16[1,3584,1024]{2,1,0:T(8,128)(2,1)} %param.10), kind=kOutput, calls=%fused_computation.6 | convolution fusion | flops 704643072 | bytes 8421376 | tf_op jit(solution)/shard_map/dot_general | solution.py:57
  48.0 11.9 %reduce-scatter.2.cloned.1.call-done = f32[96,512]{1,0:T(8,128)} async-done(((f32[96,1024]{1,0:T(8,128)}), f32[96,512]{1,0:T(8,128)}) %reduce-scatter.2.cloned.1.call-update) | async-done | bytes 196624 | tf_op jit(solution)/shard_map/reduce_scatter | solution.py:58
  59.9 1.0 multiply_convert_fusion
  60.9 5.3 %all_gather.3 = bf16[96,1024]{1,0:T(8,128)(2,1)S(1)} all-gather(bf16[96,512]{1,0:T(8,128)(2,1)S(1)} %multiply_convert_fusion), channel_id=1, replica_groups=mesh['pipe'=4,'expert'=4,'tensor'=2] {'tensor'}, dimensions={1}, use_global_device_ids=true | all-gather | bytes 294912 | tf_op jit(solution)/shard_map/all_gather | solution.py:59
  66.2 5.2 %fusion.4 = bf16[96,3584]{1,0:T(8,128)(2,1)} fusion(bf16[96,1024]{1,0:T(8,128)(2,1)S(1)} %all_gather.3, bf16[1,1024,3584]{2,1,0:T(8,128)(2,1)} %param.11), kind=kOutput, calls=%fused_computation.8 | convolution fusion | flops 704987136 | bytes 8224768 | tf_op jit(solution)/shard_map/dot_general | solution.py:60
  71.4 4.6 %all-to-all-start.1 = ((bf16[4,24,3584]{2,1,0:T(8,128)(2,1)}), bf16[4,24,3584]{2,1,0:T(8,128)(2,1)S(1)}, u32[]{:S(2)}, u32[]{:S(2)}) async-start(bf16[4,24,3584]{2,1,0:T(8,128)(2,1)} %bitcast.13), calls=%async_computation.2 | async-start | bytes 1376256 | tf_op jit(solution)/shard_map/all_to_all | solution.py:61
  76.2 1.8 %fusion.10 = f32[2,16,4]{1,2,0:T(4,128)S(1)} fusion(f32[2,16]{1,0:T(2,128)S(1)} %add_rsqrt_fusion, f32[3584]{0:T(1024)S(1)} %reduce, f32[1,3584,4]{1,2,0:T(4,128)S(1)} %copy-done, bf16[1,16,3584]{2,1,0:T(8,128)(2,1)S(1)} %collective-permute-done.1, bf16[1,16,3584]{2,1,0:T(8,128)(2,1)S(1)} %collective-permute-done), kind=kOutput, calls=%fused_computation.14 | convolution fusion | flops 5963776 | bytes 301696 | tf_op jit(solution)/shard_map/dtc,ce->dte/dot_general | solution.py:28
  78.0 4.9 %psum.15 = f32[2,16,4]{1,2,0:T(4,128)S(1)} all-reduce(f32[2,16,4]{1,2,0:T(4,128)S(1)} %fusion.10), channel_id=1, replica_groups=mesh['pipe'=4,'expert'=4,'tensor'=2] {'tensor'}, use_global_device_ids=true, to_apply=%region_2.0 | all-reduce | flops 128 | bytes 1024 | tf_op jit(solution)/shard_map/psum | solution.py:28
  82.9 1.0 gather_fusion.2
  84.3 8.4 %all-to-all-done.1 = bf16[4,24,3584]{2,1,0:T(8,128)(2,1)S(1)} async-done(((bf16[4,24,3584]{2,1,0:T(8,128)(2,1)}), bf16[4,24,3584]{2,1,0:T(8,128)(2,1)S(1)}, u32[]{:S(2)}, u32[]{:S(2)}) %all-to-all-start.1) | async-done | bytes 688160 | tf_op jit(solution)/shard_map/all_to_all | solution.py:61
  92.7 0.8 gather_fusion.1
  93.7 0.6 fusion.27
  94.3 0.7 fusion.14
  (38 shorter events, 2.0 us)
Async XLA Ops:
  6.5 69.7 %copy-start = (f32[1,3584,4]{1,2,0:T(4,128)S(1)}, f32[1,3584,4]{1,2,0:T(4,128)}, u32[]{:S(2)}) copy-start(f32[1,3584,4]{1,2,0:T(4,128)} %param.9) | copy-start | bytes 172036
  6.5 53.3 %reduce-scatter.2.cloned.1.call-start = ((), (), s32[]{:S(2)}) async-start(), calls=%async_computation.3 | async-start | bytes 589824 | tf_op jit(solution)/shard_map/reduce_scatter | solution.py:58
  7.5 6.6 %collective-permute-start = (bf16[1,16,3584]{2,1,0:T(8,128)(2,1)S(1)}, bf16[1,16,3584]{2,1,0:T(8,128)(2,1)S(1)}, u32[]{:S(2)}, u32[]{:S(2)}) collective-permute-start(bf16[1,16,3584]{2,1,0:T(8,128)(2,1)S(1)} %get-tuple-element.7), channel_id=1, source_target_pairs={{0,8},{8,16},{16,24},{24,0},{1,9},{9,17},{17,25},{25,1},{2,10},{10... | collective-permute-start | bytes 344072 | tf_op jit(solution)/shard_map/ppermute | solution.py:12
  8.1 6.1 %collective-permute-start.1 = (bf16[1,16,3584]{2,1,0:T(8,128)(2,1)S(1)}, bf16[1,16,3584]{2,1,0:T(8,128)(2,1)S(1)}, u32[]{:S(2)}, u32[]{:S(2)}) collective-permute-start(bf16[1,16,3584]{2,1,0:T(8,128)(2,1)S(1)} %get-tuple-element.8), channel_id=1, source_target_pairs={{0,24},{8,0},{16,8},{24,16},{1,25},{9,1},{17,9},{25,17},{2,26},{10... | collective-permute-start | bytes 344072 | tf_op jit(solution)/shard_map/ppermute | solution.py:12
  66.1 9.9 %copy-start.1 = (s32[2,1,16,2]{2,3,1,0:T(2,128)S(1)}, s32[2,1,16,2]{2,3,1,0:T(2,128)}, u32[]{:S(2)}) copy-start(s32[2,1,16,2]{2,3,1,0:T(2,128)} %param.7) | copy-start | bytes 772
  71.4 21.3 %all-to-all-start.1 = ((bf16[4,24,3584]{2,1,0:T(8,128)(2,1)}), bf16[4,24,3584]{2,1,0:T(8,128)(2,1)S(1)}, u32[]{:S(2)}, u32[]{:S(2)}) async-start(bf16[4,24,3584]{2,1,0:T(8,128)(2,1)} %bitcast.13), calls=%async_computation.2 | async-start | bytes 1376256 | tf_op jit(solution)/shard_map/all_to_all | solution.py:61
Sparse Core Ops, SparseCore 0:
  48.1 11.7 reduce-scatter.1
where the time goes:
time: 102 us
  blocking collectives  37.5 us (37%)
  waiting for transfers between devices  20.4 us (20%)
  between operations  13.6 us (13%)
  matrix products  12.8 us (13%)
  starting transfers between devices  7.13 us (7%)
  local copies, waits for them, and re-layouts  6.7 us (7%)
  other arithmetic  3.87 us (4%)
    all_to_all x1, blocking collectives, shards(): lax.all_to_all(outgoing, 'expert', split_axis=0, concat_axis=0, tiled=True)  22.2 us
    reduce_scatter x1, waiting for transfers between devices, shards(): share = lax.psum_scatter(inner, 'tensor', scatter_dimension=1, tiled=True)  11.9 us
    all_to_all x1, waiting for transfers between devices, shards(): lax.all_to_all(produced.reshape(senders, count, quarter), 'expert', split...  8.42 us
    all_gather x1, blocking collectives, shards(): lax.all_gather(jax.nn.silu(share).astype(jnp.bfloat16), 'tensor', axis=1,...  5.29 us
    dot_general x1, matrix products, shards(): jnp.dot(active, lower, preferred_element_type=jnp.float32)  5.25 us
    psum x1, blocking collectives, shards(): total_sq = lax.psum(squares, 'tensor')  5.16 us
    dot_general x1, matrix products, shards(): jnp.dot(received.reshape(-1, quarter), upper, preferred_element_type=jnp....  5.11 us
    psum x1, blocking collectives, shards(): lax.psum(jnp.einsum('dtc,ce->dte', normed, router[0], precision=highest),...  4.93 us
  transfers between devices with their start and end apart: 4, of which 2 were waited for; matrix products, arithmetic and copies ran while one was open for 7% of the time, Pallas kernels for 0%

commit v1 on v0

--- a/solution.py
+++ b/solution.py
@@ -1,3 +1,4 @@
+import functools
 import jax
 import jax.numpy as jnp
 from jax import lax
@@ -5,6 +6,45 @@
 
 norm_eps = 1e-06
 route_scale = 2.5
+
+
+def bench_shape(local_x, in_dim, field_in):
+    then = local_x.shape
+    passed = local_x.reshape(
+        *then[:in_dim], field_in, then[in_dim] // field_in, *then[in_dim + 1 :]
+    )
+    block_next = jnp.moveaxis(passed, in_dim, 0)
+    return block_next
+
+
+def wrap_types(x_part, axis_k):
+    x_part = jnp.moveaxis(x_part, 0, axis_k)
+    met_up = x_part.shape
+    mixed_arr = x_part.reshape(
+        *met_up[:axis_k], met_up[axis_k] * met_up[axis_k + 1], *met_up[axis_k + 2 :]
+    )
+    return mixed_arr
+
+
+def use_the_frames(unit, which_axis, q_in, vals):
+    block_last = jax.lax.axis_size(which_axis)
+    p_next = jax.lax.axis_index(which_axis)
+    shaped, front = (block_last, p_next)
+    carry_in = bench_shape(unit, q_in, shaped)
+    work_now = carry_in
+    for u in [*range(1, shaped)]:
+        extra, local_now = ((front + u) % shaped, (front - u) % shaped)
+        v1 = lax.dynamic_index_in_dim(carry_in, extra, 0)
+        by_place = []
+        for j0 in [*range(shaped)]:
+            by_place.append((j0, (j0 + u) % shaped))
+        right_arr = jax.lax.ppermute(v1, which_axis, by_place)
+        work_now = lax.dynamic_update_slice_in_dim(work_now, right_arr, local_now, axis=0)
+    v_next = wrap_types(work_now, vals)
+    return v_next
+
+
+search_wires_on = functools.partial(use_the_frames, which_axis="expert", q_in=0, vals=0)
 
 
 def shifted(x, axis, by):
@@ -58,9 +98,7 @@
     share = lax.psum_scatter(inner, "tensor", scatter_dimension=1, tiled=True)
     active = lax.all_gather(jax.nn.silu(share).astype(jnp.bfloat16), "tensor", axis=1, tiled=True)
     produced = jnp.dot(active, lower, preferred_element_type=jnp.float32).astype(jnp.bfloat16)
-    answers = lax.all_to_all(
-        produced.reshape(senders, count, quarter), "expert", split_axis=0, concat_axis=0, tiled=True
-    )
+    answers = search_wires_on(produced.reshape(senders, count, quarter))
     flat_back = answers.reshape(experts * 2 * capacity, quarter)
     gathered = (
         flat_back[target.reshape(-1)].reshape(2, tok_rows, fanout, quarter).astype(jnp.float32)

time: 102 us -> 97.3 us (0.954)
  waiting for transfers between devices: 20.4 us -> 17.3 us
    ppermute x0 -> x3, waiting for transfers between devices: none -> 12.7 us  [use_the_frames(): right_arr = jax.lax.ppermute(v1, which_axis, by_place)]
    all_to_all x1 -> x0, waiting for transfers between devices: 8.42 us -> none  [shards(): lax.all_to_all(produced.reshape(senders, count, quarter), 'expert', split...]
    reduce_scatter x1, waiting for transfers between devices: 11.9 us -> 4.16 us  [shards(): share = lax.psum_scatter(inner, 'tensor', scatter_dimension=1, tiled=True)]
    all_to_all x1 -> x0, starting transfers between devices: 4.6 us -> none  [shards(): lax.all_to_all(produced.reshape(senders, count, quarter), 'expert', split...]
    ppermute x0 -> x3, starting transfers between devices: none -> 3.7 us  [use_the_frames(): right_arr = jax.lax.ppermute(v1, which_axis, by_place)]
  transfers between devices with their start and end apart: 4 -> 6, of which waited for: 2 -> 4; matrix products, arithmetic and copies ran while one was open for 7% -> 8% of each run, Pallas kernels for 0% -> 0%
where the time goes in v1:
time: 97.3 us; the launch traced here: 96.9 us
  blocking collectives  37.1 us (38%)
  waiting for transfers between devices  17.3 us (18%)
  between operations  13.7 us (14%)
  matrix products  11.9 us (12%)
  local copies, waits for them, and re-layouts  6.82 us (7%)
  starting transfers between devices  6.16 us (6%)
  other arithmetic  3.86 us (4%)
    all_to_all x1, blocking collectives, shards(): lax.all_to_all(outgoing, 'expert', split_axis=0, concat_axis=0, tiled=True)  22 us
    ppermute x3, waiting for transfers between devices, use_the_frames(): right_arr = jax.lax.ppermute(v1, which_axis, by_place)  12.7 us
    all_gather x1, blocking collectives, shards(): lax.all_gather(jax.nn.silu(share).astype(jnp.bfloat16), 'tensor', axis=1,...  5.29 us
    dot_general x1, matrix products, shards(): jnp.dot(received.reshape(-1, quarter), upper, preferred_element_type=jnp....  5.13 us
    psum x1, blocking collectives, shards(): lax.psum(jnp.einsum('dtc,ce->dte', normed, router[0], precision=highest),...  4.93 us
    psum x1, blocking collectives, shards(): total_sq = lax.psum(squares, 'tensor')  4.92 us
    dot_general x1, matrix products, shards(): jnp.dot(active, lower, preferred_element_type=jnp.float32)  4.38 us
    reduce_scatter x1, waiting for transfers between devices, shards(): share = lax.psum_scatter(inner, 'tensor', scatter_dimension=1, tiled=True)  4.16 us
  transfers between devices with their start and end apart: 6, of which 4 were waited for; matrix products, arithmetic and copies ran while one was open for 8% of the time, Pallas kernels for 0%

profile of v1, /device:TPU:0, one launch (start us, length us, event | category | flops | bytes accessed | tf_op | source)
XLA Modules:
  0.0 96.9 jit_solution(13546419438020987189)
XLA Ops:
  6.5 1.0 %slice_bitcast_fusion.1 = (bf16[1,16,3584]{2,1,0:T(8,128)(2,1)S(1)}, bf16[1,16,3584]{2,1,0:T(8,128)(2,1)S(1)}) fusion(bf16[2,1,16,3584]{3,2,1,0:T(8,128)(2,1)} %param.6), kind=kLoop, calls=%fused_computation.25 | loop fusion | bytes 458752 | tf_op jit(solution)/shard_map/squeeze | solution.py:56
  7.5 2.5 %collective-permute-start.1 = (bf16[1,16,3584]{2,1,0:T(8,128)(2,1)S(1)}, bf16[1,16,3584]{2,1,0:T(8,128)(2,1)S(1)}, u32[]{:S(2)}, u32[]{:S(2)}) collective-permute-start(bf16[1,16,3584]{2,1,0:T(8,128)(2,1)S(1)} %get-tuple-element.11), channel_id=1, source_target_pairs={{0,24},{8,0},{16,8},{24,16},{1,25},{9,1},{17,9},{25,17},{2,26},{10... | collective-permute-start | bytes 344072 | tf_op jit(solution)/shard_map/ppermute | solution.py:52
  10.0 0.8 copy.14
  10.8 0.7 broadcast_multiply_fusion
  12.5 0.8 scatter_custom_fusion
  13.3 0.8 reduce
  14.7 4.9 %psum.14 = f32[2,16]{1,0:T(2,128)S(1)} all-reduce(f32[2,16]{1,0:T(2,128)S(1)} %multiply_reduce_fusion), channel_id=1, replica_groups=mesh['pipe'=4,'expert'=4,'tensor'=2] {'tensor'}, use_global_device_ids=true, to_apply=%region_1.0 | all-reduce | flops 32 | bytes 256 | tf_op jit(solution)/shard_map/psum | solution.py:65
  19.8 1.0 %gather_fusion = bf16[96,3584]{1,0:T(8,128)(2,1)S(1)} fusion(bf16[33,3584]{1,0:T(8,128)(2,1)S(1)} %concatenate.7, s32[1024]{0:T(1024)S(1)} %pad_clamp_fusion.1), kind=kCustom, calls=%fused_computation | custom fusion | bytes 1376640 | tf_op jit(solution)/shard_map/gather | solution.py:91
  20.8 22.0 %all_to_all.5 = bf16[4,24,3584]{2,1,0:T(8,128)(2,1)S(1)} all-to-all(bf16[4,24,3584]{2,1,0:T(8,128)(2,1)S(1)} %bitcast.65), channel_id=1, replica_groups=mesh['pipe'=4,'expert'=4,'tensor'=2] {'expert'}, dimensions={0} | all-to-all | bytes 1376256 | tf_op jit(solution)/shard_map/all_to_all | solution.py:94
  42.8 5.1 %fusion.2 = f32[96,1024]{1,0:T(8,128)} fusion(bf16[96,3584]{1,0:T(8,128)(2,1)S(1)} %bitcast.64, bf16[1,3584,1024]{2,1,0:T(8,128)(2,1)} %param.10), kind=kOutput, calls=%fused_computation.6 | convolution fusion | flops 704643072 | bytes 8421376 | tf_op jit(solution)/shard_map/dot_general | solution.py:97
  48.3 1.8 %fusion.10 = f32[2,16,4]{1,2,0:T(4,128)S(1)} fusion(f32[2,16]{1,0:T(2,128)S(1)} %add_rsqrt_fusion, f32[3584]{0:T(1024)S(1)} %reduce, f32[1,3584,4]{1,2,0:T(4,128)S(1)} %copy-done, bf16[1,16,3584]{2,1,0:T(8,128)(2,1)S(1)} %collective-permute-done.1, bf16[1,16,3584]{2,1,0:T(8,128)(2,1)S(1)} %collective-permute-done), kind=kOutput, calls=%fused_computation.14 | convolution fusion | flops 5963776 | bytes 301696 | tf_op jit(solution)/shard_map/dtc,ce->dte/dot_general | solution.py:68
  50.1 4.9 %psum.15 = f32[2,16,4]{1,2,0:T(4,128)S(1)} all-reduce(f32[2,16,4]{1,2,0:T(4,128)S(1)} %fusion.10), channel_id=1, replica_groups=mesh['pipe'=4,'expert'=4,'tensor'=2] {'tensor'}, use_global_device_ids=true, to_apply=%region_2.0 | all-reduce | flops 128 | bytes 1024 | tf_op jit(solution)/shard_map/psum | solution.py:68
  55.0 1.0 gather_fusion.2
  56.2 4.2 %reduce-scatter.2.cloned.1.call-done = f32[96,512]{1,0:T(8,128)} async-done(((f32[96,1024]{1,0:T(8,128)}), f32[96,512]{1,0:T(8,128)}) %reduce-scatter.2.cloned.1.call-update) | async-done | bytes 196624 | tf_op jit(solution)/shard_map/reduce_scatter | solution.py:98
  60.3 1.0 %multiply_convert_fusion = bf16[96,512]{1,0:T(8,128)(2,1)S(1)} fusion(f32[96,512]{1,0:T(8,128)} %reduce-scatter.2.cloned.1.call-done), kind=kLoop, calls=%fused_computation.23 | loop fusion | flops 245760 | bytes 294912 | tf_op jit(solution)/shard_map/convert_element_type | solution.py:99
  61.3 5.3 %all_gather.3 = bf16[96,1024]{1,0:T(8,128)(2,1)S(1)} all-gather(bf16[96,512]{1,0:T(8,128)(2,1)S(1)} %multiply_convert_fusion), channel_id=1, replica_groups=mesh['pipe'=4,'expert'=4,'tensor'=2] {'tensor'}, dimensions={1}, use_global_device_ids=true | all-gather | bytes 294912 | tf_op jit(solution)/shard_map/all_gather | solution.py:99
  66.6 4.4 %fusion.4 = bf16[96,3584]{1,0:T(8,128)(2,1)S(1)} fusion(bf16[96,1024]{1,0:T(8,128)(2,1)S(1)} %all_gather.3, bf16[1,1024,3584]{2,1,0:T(8,128)(2,1)} %param.11), kind=kOutput, calls=%fused_computation.8 | convolution fusion | flops 704987136 | bytes 8224768 | tf_op jit(solution)/shard_map/dot_general | solution.py:100
  71.0 1.5 %collective-permute-start.2 = (bf16[1,1,24,3584]{3,2,0,1:T(8,128)(2,1)S(1)}, bf16[1,1,24,3584]{3,2,0,1:T(8,128)(2,1)S(1)}, u32[]{:S(2)}, u32[]{:S(2)}) collective-permute-start(bf16[1,1,24,3584]{3,2,0,1:T(8,128)(2,1)S(1)} %constant_dynamic-slice_fusion.2), channel_id=1, source_target_pairs={{0,2},{2,4},{4,6},{6,0},{1,3},{3,5},{5,7},{7,1},{8,10},{10,12},{12... | collective-permute-start | bytes 516104 | tf_op jit(solution)/shard_map/ppermute | solution.py:41
  72.6 5.7 %collective-permute-done.2 = bf16[1,1,24,3584]{3,2,0,1:T(8,128)(2,1)S(1)} collective-permute-done((bf16[1,1,24,3584]{3,2,0,1:T(8,128)(2,1)S(1)}, bf16[1,1,24,3584]{3,2,0,1:T(8,128)(2,1)S(1)}, u32[]{:S(2)}, u32[]{:S(2)}) %collective-permute-start.2) | collective-permute-done | bytes 172064 | tf_op jit(solution)/shard_map/ppermute | solution.py:41
  78.3 0.7 collective-permute-start.3
  79.1 1.5 %collective-permute-start.4 = (bf16[1,1,24,3584]{3,2,0,1:T(8,128)(2,1)S(1)}, bf16[1,1,24,3584]{3,2,0,1:T(8,128)(2,1)S(1)}, u32[]{:S(2)}, u32[]{:S(2)}) collective-permute-start(bf16[1,1,24,3584]{3,2,0,1:T(8,128)(2,1)S(1)} %get-tuple-element.7), channel_id=1, source_target_pairs={{0,6},{2,0},{4,2},{6,4},{1,7},{3,1},{5,3},{7,5},{8,14},{10,8},{12,... | collective-permute-start | bytes 516104 | tf_op jit(solution)/shard_map/ppermute | solution.py:41
  80.6 7.0 %collective-permute-done.3 = bf16[1,1,24,3584]{3,2,0,1:T(8,128)(2,1)S(1)} collective-permute-done((bf16[1,1,24,3584]{3,2,0,1:T(8,128)(2,1)S(1)}, bf16[1,1,24,3584]{3,2,0,1:T(8,128)(2,1)S(1)}, u32[]{:S(2)}, u32[]{:S(2)}) %collective-permute-start.3) | collective-permute-done | bytes 172064 | tf_op jit(solution)/shard_map/ppermute | solution.py:41
  87.7 0.8 gather_fusion.1
  89.3 0.7 fusion.14
  (46 shorter events, 3.3 us)
Async XLA Ops:
  6.5 41.8 %copy-start = (f32[1,3584,4]{1,2,0:T(4,128)S(1)}, f32[1,3584,4]{1,2,0:T(4,128)}, u32[]{:S(2)}) copy-start(f32[1,3584,4]{1,2,0:T(4,128)} %param.9) | copy-start | bytes 172036
  6.5 53.8 %reduce-scatter.2.cloned.1.call-start = ((), (), s32[]{:S(2)}) async-start(), calls=%async_computation.2 | async-start | bytes 589824 | tf_op jit(solution)/shard_map/reduce_scatter | solution.py:98
  7.5 6.6 %collective-permute-start.1 = (bf16[1,16,3584]{2,1,0:T(8,128)(2,1)S(1)}, bf16[1,16,3584]{2,1,0:T(8,128)(2,1)S(1)}, u32[]{:S(2)}, u32[]{:S(2)}) collective-permute-start(bf16[1,16,3584]{2,1,0:T(8,128)(2,1)S(1)} %get-tuple-element.11), channel_id=1, source_target_pairs={{0,24},{8,0},{16,8},{24,16},{1,25},{9,1},{17,9},{25,17},{2,26},{10... | collective-permute-start | bytes 344072 | tf_op jit(solution)/shard_map/ppermute | solution.py:52
  10.0 4.6 %collective-permute-start = (bf16[1,16,3584]{2,1,0:T(8,128)(2,1)S(1)}, bf16[1,16,3584]{2,1,0:T(8,128)(2,1)S(1)}, u32[]{:S(2)}, u32[]{:S(2)}) collective-permute-start(bf16[1,16,3584]{2,1,0:T(8,128)(2,1)S(1)} %get-tuple-element.10), channel_id=1, source_target_pairs={{0,8},{8,16},{16,24},{24,0},{1,9},{9,17},{17,25},{25,1},{2,10},{10... | collective-permute-start | bytes 344072 | tf_op jit(solution)/shard_map/ppermute | solution.py:52
  42.8 5.2 %copy-start.1 = (s32[2,1,16,2]{2,3,1,0:T(2,128)S(1)}, s32[2,1,16,2]{2,3,1,0:T(2,128)}, u32[]{:S(2)}) copy-start(s32[2,1,16,2]{2,3,1,0:T(2,128)} %param.7) | copy-start | bytes 772
  71.0 7.3 %collective-permute-start.2 = (bf16[1,1,24,3584]{3,2,0,1:T(8,128)(2,1)S(1)}, bf16[1,1,24,3584]{3,2,0,1:T(8,128)(2,1)S(1)}, u32[]{:S(2)}, u32[]{:S(2)}) collective-permute-start(bf16[1,1,24,3584]{3,2,0,1:T(8,128)(2,1)S(1)} %constant_dynamic-slice_fusion.2), channel_id=1, source_target_pairs={{0,2},{2,4},{4,6},{6,0},{1,3},{3,5},{5,7},{7,1},{8,10},{10,12},{12... | collective-permute-start | bytes 516104 | tf_op jit(solution)/shard_map/ppermute | solution.py:41
  78.3 9.3 %collective-permute-start.3 = (bf16[1,1,24,3584]{3,2,0,1:T(8,128)(2,1)S(1)}, bf16[1,1,24,3584]{3,2,0,1:T(8,128)(2,1)S(1)}, u32[]{:S(2)}, u32[]{:S(2)}) collective-permute-start(bf16[1,1,24,3584]{3,2,0,1:T(8,128)(2,1)S(1)} %get-tuple-element.8), channel_id=1, source_target_pairs={{0,4},{2,6},{4,0},{6,2},{1,5},{3,7},{5,1},{7,3},{8,12},{10,14},{12... | collective-permute-start | bytes 516104 | tf_op jit(solution)/shard_map/ppermute | solution.py:41
  79.1 8.5 %collective-permute-start.4 = (bf16[1,1,24,3584]{3,2,0,1:T(8,128)(2,1)S(1)}, bf16[1,1,24,3584]{3,2,0,1:T(8,128)(2,1)S(1)}, u32[]{:S(2)}, u32[]{:S(2)}) collective-permute-start(bf16[1,1,24,3584]{3,2,0,1:T(8,128)(2,1)S(1)} %get-tuple-element.7), channel_id=1, source_target_pairs={{0,6},{2,0},{4,2},{6,4},{1,7},{3,1},{5,3},{7,5},{8,14},{10,8},{12,... | collective-permute-start | bytes 516104 | tf_op jit(solution)/shard_map/ppermute | solution.py:41
Sparse Core Ops, SparseCore 0:
  48.1 12.2 reduce-scatter.1
